TPU v7x, 32 devices: a whole 2x2x4 slice. The times are simulated.
32 devices in a mesh: grp: 2 (over y), sv: 4 (over z), tv: 4 (over x, core).
Axes of the slice: x: 2, y: 2, z: 4, core: 2. Of those that a mesh axis runs over, the one named last changes fastest.
Arguments:
- student_states: bfloat16 [512, 1792], P('grp', 'tv'), parts along dimension 0, may hold values from -60 to 60
- teacher_states: bfloat16 [512, 2304], P('grp', 'tv'), parts along dimension 0, may hold values from -60 to 60
- student_queries: bfloat16 [512, 256], P('grp', 'tv'), parts along dimension 0, may hold values from -60 to 60
- teacher_keys: bfloat16 [512, 256], P('grp', 'tv'), parts along dimension 0, may hold values from -6 to 6
- student_targets: int32 [512], P('grp'), parts along dimension 0, may hold values from 0 to 8191
- teacher_targets: int32 [512], P('grp'), parts along dimension 0, may hold values from 0 to 8191
- student_lengths: int32 [4], P('grp'), parts along dimension 0, may hold values from 64 to 128
- teacher_lengths: int32 [4], P('grp'), parts along dimension 0, may hold values from 64 to 128
- to_teacher: bfloat16 [1792, 2304], P('tv', 'sv'), may hold values from -0.125 to 0.125
- to_student: bfloat16 [2304, 1792], P('tv', 'sv'), may hold values from -0.125 to 0.125
- student_head: bfloat16 [1792, 8192], P(None, ('sv', 'tv')), may hold values from -0.125 to 0.125
- teacher_head: bfloat16 [2304, 8192], P(None, ('sv', 'tv')), may hold values from -0.125 to 0.125
Outputs:
- student_loss: float32 [512], P('grp'), parts along dimension 0
- teacher_loss: float32 [512], P('grp'), parts along dimension 0
- student_grad: bfloat16 [512, 8192], P('grp', ('sv', 'tv')), parts along dimension 0
- teacher_grad: bfloat16 [512, 8192], P('grp', ('sv', 'tv')), parts along dimension 0
There are 2 independent parts, one for each index of `grp`. A program takes and returns all parts, laid end to end along the dimension named above; an argument that names none is the same for every part. Nothing has to cross between parts.
All inputs are finite; a program needn't handle non-finite values.
Results may differ from a plain program's by a relative error of at most 0.0086.
Values may be sent and summed in bfloat16 or wider, within the bound.
No kernel may reach another device: no remote copies, remote signals or barrier semaphores. Data moves between devices by JAX's collectives and lax.ppermute only.
A program may use at most 64 MiB of HBM per device.

v0:
```python
import jax
import jax.numpy as jnp
from jax import lax
from jax.sharding import PartitionSpec as P

DK = 256
floor_value = -1e30


def combined_all(part, axis, combine):
    gathered = jax.tree.map(lambda a: lax.all_gather(a, axis), part)

    def take(source):
        return jax.tree.map(lambda a: lax.dynamic_index_in_dim(a, source, 0, False), gathered)

    return lax.fori_loop(
        1, lax.axis_size(axis), lambda source, state: combine(state, take(source)), take(0)
    )


def align_block(student_queries, teacher_keys, teacher_states, teacher_lengths):
    sequences = teacher_lengths.shape[0]
    query_cols = student_queries.shape[1]
    queries = student_queries.reshape(sequences, -1, query_cols)
    keyset = teacher_keys.reshape(sequences, -1, query_cols)
    partial_scores = jnp.einsum("sid,sjd->sij", queries, keyset, preferred_element_type=jnp.float32)
    scores = lax.psum(partial_scores, "tv") * DK ** (-0.5)
    positions = lax.broadcasted_iota(jnp.int32, scores.shape, 2)
    scores = jnp.where(positions < teacher_lengths[:, None, None], scores, floor_value)
    highest = jnp.max(scores, axis=2, keepdims=True)
    weights = jnp.exp(scores - highest)
    weights = (weights / jnp.sum(weights, axis=2, keepdims=True)).astype(jnp.bfloat16)
    states = teacher_states.reshape(sequences, -1, teacher_states.shape[1])
    aligned = jnp.einsum("sij,sjd->sid", weights, states, preferred_element_type=jnp.float32)
    return aligned.astype(jnp.bfloat16).reshape(-1, teacher_states.shape[1])


def live_rows(row_count, lengths, sequence_length):
    indices = lax.broadcasted_iota(jnp.int32, (row_count,), 0)
    sequence = indices // sequence_length
    position = indices % sequence_length
    owners = lax.broadcasted_iota(jnp.int32, (row_count, lengths.shape[0]), 1)
    length_limit = jnp.sum(jnp.where(sequence[:, None] == owners, lengths[None, :], 0), axis=1)
    return (position < length_limit).astype(jnp.float32)


def local_stats(logits, target_cols, kind_index):
    other_kind = 1 - kind_index
    highest = jnp.max(logits, axis=2)
    scaled = jnp.exp(logits - highest[:, :, None])
    totals = jnp.sum(scaled, axis=2)
    spread = jnp.sum(
        scaled[:, kind_index] * (logits[:, kind_index] - logits[:, other_kind]), axis=1
    )
    column = lax.broadcasted_iota(jnp.int32, logits.shape, 2)
    picked = jnp.sum(jnp.where(column == target_cols[:, None, None], logits, 0.0), axis=2)
    return (highest, totals, spread, picked)


def side_combine(former, latter, kind_index):
    highest = jnp.maximum(former[0], latter[0])
    former_scale = jnp.exp(former[0] - highest)
    latter_scale = jnp.exp(latter[0] - highest)
    totals = former[1] * former_scale + latter[1] * latter_scale
    spread = former[2] * former_scale[:, kind_index] + latter[2] * latter_scale[:, kind_index]
    return (highest, totals, spread, former[3] + latter[3])


def student_combine(former, latter):
    return side_combine(former, latter, 1)


def teacher_combine(former, latter):
    return side_combine(former, latter, 0)


def side_terms(logits, statistics, target_cols):
    highest, totals = (statistics[0], statistics[1])
    log_total = highest + jnp.log(totals)
    chances = jnp.exp(logits - log_total[:, :, None])
    column = lax.broadcasted_iota(jnp.int32, chances[:, 0].shape, 1)
    target_hot = (column == target_cols[:, None]).astype(jnp.float32)
    return (log_total, chances, target_hot)


def student_side(logits, statistics, target_cols, live_mask):
    log_total, chances, target_hot = side_terms(logits, statistics, target_cols)
    totals, spread, picked = (statistics[1], statistics[2], statistics[3])
    diverge = spread / totals[:, 1] - log_total[:, 1] + log_total[:, 0]
    row_loss = live_mask * (
        log_total[:, 0] - picked[:, 0] + log_total[:, 1] - picked[:, 1] + diverge
    )
    gradient = live_mask[:, None] * (2.0 * chances[:, 0] - target_hot - chances[:, 1])
    return (row_loss, gradient.astype(jnp.bfloat16))


def teacher_side(logits, statistics, target_cols, live_mask):
    log_total, chances, target_hot = side_terms(logits, statistics, target_cols)
    totals, spread, picked = (statistics[1], statistics[2], statistics[3])
    diverge = spread / totals[:, 0] - log_total[:, 0] + log_total[:, 1]
    row_loss = live_mask * (diverge + log_total[:, 1] - picked[:, 1])
    gradient = live_mask[:, None] * (2.0 * chances[:, 1] - chances[:, 0] - target_hot)
    return (row_loss, gradient.astype(jnp.bfloat16))


def body(
    student_states,
    teacher_states,
    student_queries,
    teacher_keys,
    student_targets,
    teacher_targets,
    student_lengths,
    teacher_lengths,
    to_teacher,
    to_student,
    student_head,
    teacher_head,
):
    row_total = student_states.shape[0]
    sequence_length = row_total // student_lengths.shape[0]
    sv_index = lax.axis_index("sv")
    tv_index = lax.axis_index("tv")
    tv_count = lax.axis_size("tv")
    vocab_block = sv_index * tv_count + tv_index
    aligned_block = align_block(student_queries, teacher_keys, teacher_states, teacher_lengths)
    full_student = lax.all_gather(student_states, "tv", axis=1, tiled=True)
    full_aligned = lax.all_gather(aligned_block, "tv", axis=1, tiled=True)
    teacher_part = lax.psum(
        jnp.dot(student_states, to_teacher, preferred_element_type=jnp.float32), "tv"
    )
    student_part = lax.psum(
        jnp.dot(aligned_block, to_student, preferred_element_type=jnp.float32), "tv"
    )
    into_teacher = lax.all_gather(teacher_part.astype(jnp.bfloat16), "sv", axis=1, tiled=True)
    into_student = lax.all_gather(student_part.astype(jnp.bfloat16), "sv", axis=1, tiled=True)
    student_logits = jnp.stack(
        [
            jnp.dot(full_student, student_head, preferred_element_type=jnp.float32),
            jnp.dot(into_student, student_head, preferred_element_type=jnp.float32),
        ],
        axis=1,
    )
    student_cols = student_targets - vocab_block * student_head.shape[1]
    student_stats = local_stats(student_logits, student_cols, 1)
    teacher_logits = jnp.stack(
        [
            jnp.dot(full_aligned, teacher_head, preferred_element_type=jnp.float32),
            jnp.dot(into_teacher, teacher_head, preferred_element_type=jnp.float32),
        ],
        axis=1,
    )
    teacher_cols = teacher_targets - vocab_block * teacher_head.shape[1]
    teacher_stats = local_stats(teacher_logits, teacher_cols, 0)
    student_stats = combined_all(student_stats, ("sv", "tv"), student_combine)
    teacher_stats = combined_all(teacher_stats, ("sv", "tv"), teacher_combine)
    every_live = live_rows(row_total, student_lengths, sequence_length)
    student_loss, student_grad = student_side(
        student_logits, student_stats, student_cols, every_live
    )
    teacher_loss, teacher_grad = teacher_side(
        teacher_logits, teacher_stats, teacher_cols, every_live
    )
    return (student_loss, teacher_loss, student_grad, teacher_grad)


def solution(mesh):
    in_specs = (
        P("grp", "tv"),
        P("grp", "tv"),
        P("grp", "tv"),
        P("grp", "tv"),
        P("grp"),
        P("grp"),
        P("grp"),
        P("grp"),
        P("tv", "sv"),
        P("tv", "sv"),
        P(None, ("sv", "tv")),
        P(None, ("sv", "tv")),
    )
    out_specs = (P("grp"), P("grp"), P("grp", ("sv", "tv")), P("grp", ("sv", "tv")))
    return jax.shard_map(body, mesh=mesh, in_specs=in_specs, out_specs=out_specs, check_vma=False)
```

profile of v0, /device:TPU:0, one launch (start us, length us, event | category | flops | bytes accessed | tf_op | source)
XLA Modules:
  0.0 294.7 jit_solution(5090712872728876629)
XLA Ops:
  7.2 0.0 copy-start
  7.2 0.0 copy-start.5
  7.2 0.0 copy-start.15
  7.2 0.0 copy-start.16
  7.2 0.0 copy-start.17
  7.2 0.0 all-reduce.4.cloned.1.call-start
  7.3 1.8 fusion.30
  9.1 0.0 all-reduce.4.cloned.1.call-update
  9.1 0.0 all-gather.15.cloned.1.call-start
  9.2 12.4 %all_gather.60 = bf16[256,1792]{0,1:T(8,128)(2,1)} all-gather(bf16[256,448]{0,1:T(8,128)(2,1)} %param.16), channel_id=1, replica_groups=mesh['grp'=2,'sv'=4,'tv'=4] {'tv'}, dimensions={1}, use_global_device_ids=true | all-gather | bytes 1146880 | tf_op jit(solution)/shard_map/all_gather | solution.py:127
  21.6 1.3 fusion.60
  22.9 0.0 copy-done.15
  22.9 0.0 copy-done.16
  22.9 0.0 copy-done.17
  23.0 0.1 fusion.35
  23.0 22.0 %all-reduce.4.cloned.1.call-done = f32[2,128,128]{2,1,0:T(8,128)} async-done(((f32[2,128,128]{2,1,0:T(8,128)}), f32[2,128,128]{2,1,0:T(8,128)}) %all-reduce.4.cloned.1.call-update) | async-done | bytes 131088 | tf_op jit(solution)/shard_map/psum | solution.py:27
  45.1 1.2 fusion.56
  46.3 2.4 fusion.5
  48.7 1.5 fusion.48
  50.1 26.0 %all-reduce.5 = (bf16[256,448]{0,1:T(8,128)(2,1)}, bf16[256,576]{0,1:T(8,128)(2,1)}) all-reduce(f32[256,448]{0,1:T(8,128)S(1)} %fusion.48, f32[256,576]{0,1:T(8,128)S(1)} %fusion.60), channel_id=1, replica_groups=mesh['grp'=2,'sv'=4,'tv'=4] {'tv'}, use_global_device_ids=true, to_apply=%region_4.5 | all-reduce | flops 262144 | bytes 1572864 | tf_op jit(solution)/shard_map/psum | solution.py:132
  76.2 0.0 all-gather.15.cloned.1.call-update
  76.2 0.0 all-gather.13.cloned.1.call-start
  76.2 0.6 fusion.47
  76.8 2.6 fusion.57
  79.4 0.8 copy.53
  80.2 33.6 %all_gather.61 = bf16[256,1792]{0,1:T(8,128)(2,1)S(1)} all-gather(bf16[256,448]{0,1:T(8,128)(2,1)S(1)} %copy-done.6), channel_id=1, replica_groups=mesh['grp'=2,'sv'=4,'tv'=4] {'sv'}, dimensions={1}, use_global_device_ids=true | all-gather | bytes 1146880 | tf_op jit(solution)/shard_map/all_gather | solution.py:136
  113.8 0.7 fusion.58
  114.5 0.4 select_reduce_fusion.1
  114.8 0.3 fusion.52
  115.1 0.2 fusion.20
  115.3 20.8 %all-gather.8 = f32[16,1,256]{2,1,0:T(1,128)S(1)} all-gather(f32[1,1,256]{2,1,0:T(1,128)S(1)} %bitcast.187), channel_id=4, replica_groups=mesh['grp'=2,'sv'=4,'tv'=4] {'sv','tv'}, dimensions={0}, use_global_device_ids=true | all-gather | bytes 17408 | tf_op jit(solution)/shard_map/all_gather | solution.py:11
  136.1 17.5 %all-gather = f32[4096,2]{0,1:T(2,128)S(1)} all-gather(f32[256,2]{0,1:T(2,128)S(1)} %get-tuple-element.461), channel_id=2, replica_groups=mesh['grp'=2,'sv'=4,'tv'=4] {'sv','tv'}, dimensions={0}, use_global_device_ids=true | all-gather | bytes 34816 | tf_op jit(solution)/shard_map/all_gather | solution.py:11
  153.6 18.9 %all-gather.1 = f32[4096,2]{0,1:T(2,128)S(1)} all-gather(f32[256,2]{0,1:T(2,128)S(1)} %get-tuple-element.510), channel_id=3, replica_groups=mesh['grp'=2,'sv'=4,'tv'=4] {'sv','tv'}, dimensions={0}, use_global_device_ids=true | all-gather | bytes 34816 | tf_op jit(solution)/shard_map/all_gather | solution.py:11
  172.4 17.5 %all-gather.3 = f32[4096,2]{0,1:T(2,128)S(1)} all-gather(f32[256,2]{0,1:T(2,128)S(1)} %get-tuple-element.460), channel_id=5, replica_groups=mesh['grp'=2,'sv'=4,'tv'=4] {'sv','tv'}, dimensions={0}, use_global_device_ids=true | all-gather | bytes 34816 | tf_op jit(solution)/shard_map/all_gather | solution.py:11
  189.9 0.0 all-gather.13.cloned.1.call-update
  189.9 1.6 while.42
  191.5 0.6 slice.101
  192.1 0.6 fusion.55
  192.7 0.6 fusion.54
  193.3 2.9 fusion.61
  196.2 9.7 %all-gather.13.cloned.1.call-done = bf16[256,2304]{0,1:T(8,128)(2,1)} async-done(((bf16[256,576]{0,1:T(8,128)(2,1)}), bf16[256,2304]{0,1:T(8,128)(2,1)}) %all-gather.13.cloned.1.call-update) | async-done | bytes 1179664 | tf_op jit(solution)/shard_map/all_gather | solution.py:128
  205.9 2.1 fusion.59
  208.0 0.0 copy-start.2
  208.1 0.0 copy-done.1
  208.1 0.4 select_reduce_fusion
  208.4 20.5 %all-gather.4 = f32[4096,2]{0,1:T(2,128)S(1)} all-gather(f32[256,2]{0,1:T(2,128)S(1)} %get-tuple-element.459), channel_id=6, replica_groups=mesh['grp'=2,'sv'=4,'tv'=4] {'sv','tv'}, dimensions={0}, use_global_device_ids=true | all-gather | bytes 34816 | tf_op jit(solution)/shard_map/all_gather | solution.py:11
  228.9 0.3 fusion.51
  229.2 0.2 fusion.18
  229.4 0.0 copy-done.2
  229.4 17.4 %all-gather.9 = f32[16,1,256]{2,1,0:T(1,128)S(1)} all-gather(f32[1,1,256]{2,1,0:T(1,128)S(1)} %bitcast.188), channel_id=8, replica_groups=mesh['grp'=2,'sv'=4,'tv'=4] {'sv','tv'}, dimensions={0}, use_global_device_ids=true | all-gather | bytes 17408 | tf_op jit(solution)/shard_map/all_gather | solution.py:11
  246.8 18.8 %all-gather.5 = f32[4096,2]{0,1:T(2,128)S(1)} all-gather(f32[256,2]{0,1:T(2,128)S(1)} %get-tuple-element.508), channel_id=7, replica_groups=mesh['grp'=2,'sv'=4,'tv'=4] {'sv','tv'}, dimensions={0}, use_global_device_ids=true | all-gather | bytes 34816 | tf_op jit(solution)/shard_map/all_gather | solution.py:11
  265.7 17.5 %all-gather.7 = f32[4096,2]{0,1:T(2,128)S(1)} all-gather(f32[256,2]{0,1:T(2,128)S(1)} %get-tuple-element.458), channel_id=9, replica_groups=mesh['grp'=2,'sv'=4,'tv'=4] {'sv','tv'}, dimensions={0}, use_global_device_ids=true | all-gather | bytes 34816 | tf_op jit(solution)/shard_map/all_gather | solution.py:11
  283.2 1.6 while.43
  284.8 0.0 copy-start.9
  284.8 1.5 subtract_exponential_fusion.2
  286.4 0.0 copy-start.8
  286.4 0.0 copy-start.10
  286.4 0.0 copy-start.11
  286.4 1.1 fusion.11
  287.5 0.0 copy-done.11
  287.5 0.0 copy-done.12
  287.6 0.0 copy-done.13
  287.6 0.0 copy-done.14
  287.6 0.6 fusion.37
  (188 shorter events, 1.9 us)
Async XLA Ops:
  7.2 186.1 %copy-start = (bf16[2304,512]{1,0:T(8,128)(2,1)S(1)}, bf16[2304,512]{1,0:T(8,128)(2,1)}, u32[]{:S(2)}) copy-start(bf16[2304,512]{1,0:T(8,128)(2,1)} %param.27) | copy-start | bytes 7077892
  7.2 14.4 %copy-start.5 = (bf16[448,576]{1,0:T(8,128)(2,1)S(1)}, bf16[448,576]{1,0:T(8,128)(2,1)}, u32[]{:S(2)}) copy-start(bf16[448,576]{1,0:T(8,128)(2,1)} %param.24) | copy-start | bytes 1548292
  7.2 15.7 %copy-start.15 = (s32[256]{0:T(256)S(1)}, s32[256]{0:T(256)}, u32[]{:S(2)}) copy-start(s32[256]{0:T(256)} %param.21) | copy-start | bytes 3076
  7.2 15.7 %copy-start.16 = (s32[256]{0:T(256)S(1)}, s32[256]{0:T(256)}, u32[]{:S(2)}) copy-start(s32[256]{0:T(256)} %param.20) | copy-start | bytes 3076
  7.2 15.7 %copy-start.17 = (s32[2]{0:T(128)S(1)}, s32[2]{0:T(128)}, u32[]{:S(2)}) copy-start(s32[2]{0:T(128)} %param.22) | copy-start | bytes 28
  7.2 37.9 %copy-start.18 = (s32[2]{0:T(128)S(1)}, s32[2]{0:T(128)}, u32[]{:S(2)}) copy-start(s32[2]{0:T(128)} %param.23) | copy-start | bytes 28
  7.2 37.9 %all-reduce.4.cloned.1.call-start = ((), (), s32[]{:S(2)}) async-start(), calls=%async_computation | async-start | bytes 262144 | tf_op jit(solution)/shard_map/psum | solution.py:27
  9.1 184.2 %all-gather.15.cloned.1.call-start = ((), (), s32[]{:S(2)}) async-start(), calls=%async_computation.2 | async-start | bytes 1474560 | tf_op jit(solution)/shard_map/all_gather | solution.py:135
  23.0 53.2 %copy-start.7 = (s32[256]{0:T(256)}, s32[256]{0:T(256)S(1)}, u32[]{:S(2)}) copy-start(s32[256]{0:T(256)S(1)} %fusion.35) | copy-start | bytes 3076
  76.2 3.2 %copy-start.4 = (bf16[2,72,8,128]{3,2,1,0:T(8,128)(2,1)S(1)}, bf16[2,72,8,128]{3,2,1,0:T(8,128)(2,1)}, u32[]{:S(2)}) copy-start(bf16[2,72,8,128]{3,2,1,0:T(8,128)(2,1)} %fusion.5) | copy-start | bytes 884740
  76.2 129.7 %all-gather.13.cloned.1.call-start = ((), (), s32[]{:S(2)}) async-start(), calls=%async_computation.1 | async-start | bytes 1474560 | tf_op jit(solution)/shard_map/all_gather | solution.py:128
  76.8 3.4 %copy-start.6 = (bf16[256,448]{0,1:T(8,128)(2,1)S(1)}, bf16[256,448]{0,1:T(8,128)(2,1)}, u32[]{:S(2)}) copy-start(bf16[256,448]{0,1:T(8,128)(2,1)} %get-tuple-element.498) | copy-start | bytes 688132
  76.8 37.0 %copy-start.3 = (bf16[1792,512]{1,0:T(8,128)(2,1)S(1)}, bf16[1792,512]{1,0:T(8,128)(2,1)}, u32[]{:S(2)}) copy-start(bf16[1792,512]{1,0:T(8,128)(2,1)} %param.26) | copy-start | bytes 5505028
  205.9 2.1 copy-start.1
  208.0 21.3 %copy-start.2 = (f32[256,512]{1,0:T(8,128)}, f32[256,512]{1,0:T(8,128)S(1)}, u32[]{:S(2)}) copy-start(f32[256,512]{1,0:T(8,128)S(1)} %fusion.59) | copy-start | bytes 1572868
  284.8 1.6 copy-start.9
  286.4 1.2 copy-start.8
  286.4 1.2 copy-start.10
  286.4 1.2 copy-start.11
  286.4 1.2 copy-start.12
  286.4 1.2 copy-start.13
  286.4 1.2 copy-start.14
Sparse Core Ops, SparseCore 0:
  11.0 34.0 all-reduce.3
  76.3 43.0 all-gather.14
  190.0 15.8 all-gather.12
where the time goes:
time: 295 us
  blocking collectives  221 us (75%)
  waiting for transfers between devices  31.8 us (11%)
  matrix products  15.3 us (5%)
  between operations  14.1 us (5%)
  other arithmetic  8 us (3%)
  local copies, waits for them, and re-layouts  3.24 us (1%)
    all_gather x8, blocking collectives, combined_all(): gathered = jax.tree.map(lambda a: lax.all_gather(a, axis), part)  149 us
    all_gather x1, blocking collectives, body(): lax.all_gather(student_part.astype(jnp.bfloat16), 'sv', axis=1, tiled=True)  33.6 us
    psum x1, blocking collectives, body(): lax.psum(jnp.dot(aligned_block, to_student, preferred_element_type=jnp.fl...  26 us
    psum x1, waiting for transfers between devices, align_block(): scores = lax.psum(partial_scores, 'tv') * DK ** (-0.5)  22 us
    all_gather x1, blocking collectives, body(): full_student = lax.all_gather(student_states, 'tv', axis=1, tiled=True)  12.4 us
    all_gather x1, waiting for transfers between devices, body(): full_aligned = lax.all_gather(aligned_block, 'tv', axis=1, tiled=True)  9.69 us
  transfers between devices with their start and end apart: 3, of which 2 were waited for; matrix products, arithmetic and copies ran while one was open for 4% of the time, Pallas kernels for 0%

commit v1 on v0

--- a/solution.py
+++ b/solution.py
@@ -125,7 +125,15 @@
     vocab_block = sv_index * tv_count + tv_index
     aligned_block = align_block(student_queries, teacher_keys, teacher_states, teacher_lengths)
     full_student = lax.all_gather(student_states, "tv", axis=1, tiled=True)
-    full_aligned = lax.all_gather(aligned_block, "tv", axis=1, tiled=True)
+    n_parts = jax.lax.axis_size("tv")
+    by_rank = [aligned_block]
+    for b in range(n_parts - 1):
+        tall = jax.lax.ppermute(
+            by_rank[-1], axis_name="tv", perm=[(rr, (rr + 1) % n_parts) for rr in range(n_parts)]
+        )
+        by_rank.append(tall)
+    aux = jnp.concatenate(by_rank[::-1], axis=1)
+    full_aligned = jnp.roll(aux, (jax.lax.axis_index("tv") + 1) * aligned_block.shape[1], axis=1)
     teacher_part = lax.psum(
         jnp.dot(student_states, to_teacher, preferred_element_type=jnp.float32), "tv"
     )

time: 295 us -> 285 us (0.966)
  blocking collectives: 221 us -> 208 us
  local copies, waits for them, and re-layouts: 3.24 us -> 8.24 us
  waiting for transfers between devices: 31.8 us -> 27.1 us
    all_gather x1, blocking collectives: 33.6 us -> 21.2 us  [body(): lax.all_gather(student_part.astype(jnp.bfloat16), 'sv', axis=1, tiled=True)]
    all_gather x1 -> x0, waiting for transfers between devices: 9.69 us -> none  [body(): full_aligned = lax.all_gather(aligned_block, 'tv', axis=1, tiled=True)]
    ppermute x0 -> x3, waiting for transfers between devices: none -> 9.16 us  [body(): jax.lax.ppermute(by_rank[-1], axis_name='tv', perm=[(rr, (rr + 1) % n_par...]
    unnamed x40 -> x43, local copies, waits for them, and re-layouts: 0.09 us -> 5.05 us
    psum x1, waiting for transfers between devices: 22 us -> 17.9 us  [align_block(): scores = lax.psum(partial_scores, 'tv') * DK ** (-0.5)]
  transfers between devices with their start and end apart: 3 -> 5, of which waited for: 2 -> 3; matrix products, arithmetic and copies ran while one was open for 4% -> 6% of each run, Pallas kernels for 0% -> 0%
where the time goes in v1:
time: 285 us; the launch traced here: 284 us
  blocking collectives  208 us (73%)
  waiting for transfers between devices  27.1 us (10%)
  matrix products  16.3 us (6%)
  between operations  14.4 us (5%)
  other arithmetic  8.67 us (3%)
  local copies, waits for them, and re-layouts  8.24 us (3%)
    all_gather x8, blocking collectives, combined_all(): gathered = jax.tree.map(lambda a: lax.all_gather(a, axis), part)  147 us
    psum x1, blocking collectives, body(): lax.psum(jnp.dot(aligned_block, to_student, preferred_element_type=jnp.fl...  27.4 us
    all_gather x1, blocking collectives, body(): lax.all_gather(student_part.astype(jnp.bfloat16), 'sv', axis=1, tiled=True)  21.2 us
    psum x1, waiting for transfers between devices, align_block(): scores = lax.psum(partial_scores, 'tv') * DK ** (-0.5)  17.9 us
    all_gather x1, blocking collectives, body(): full_student = lax.all_gather(student_states, 'tv', axis=1, tiled=True)  12.4 us
    ppermute x3, waiting for transfers between devices, body(): jax.lax.ppermute(by_rank[-1], axis_name='tv', perm=[(rr, (rr + 1) % n_par...  9.16 us
  transfers between devices with their start and end apart: 5, of which 3 were waited for; matrix products, arithmetic and copies ran while one was open for 6% of the time, Pallas kernels for 0%

profile of v1, /device:TPU:0, one launch (start us, length us, event | category | flops | bytes accessed | tf_op | source)
XLA Modules:
  0.0 284.3 jit_solution(8702338200053395282)
XLA Ops:
  7.2 0.0 copy-start
  7.2 0.0 copy-start.12
  7.2 0.0 copy-start.13
  7.2 0.0 copy-start.14
  7.2 0.0 all-reduce.4.cloned.1.call-start
  7.3 1.8 fusion.32
  9.1 0.0 all-reduce.4.cloned.1.call-update
  9.1 0.0 all-gather.12.cloned.1.call-start
  9.2 12.4 %all_gather.57 = bf16[256,1792]{0,1:T(8,128)(2,1)} all-gather(bf16[256,448]{0,1:T(8,128)(2,1)} %param.16), channel_id=1, replica_groups=mesh['grp'=2,'sv'=4,'tv'=4] {'tv'}, dimensions={1}, use_global_device_ids=true | all-gather | bytes 1146880 | tf_op jit(solution)/shard_map/all_gather | solution.py:127
  21.5 2.4 fusion.62
  24.0 0.0 copy-done.14
  24.0 0.1 fusion.37
  24.1 2.4 fusion.60
  26.5 0.6 fusion.50
  27.1 17.9 %all-reduce.4.cloned.1.call-done = f32[2,128,128]{2,1,0:T(8,128)} async-done(((f32[2,128,128]{2,1,0:T(8,128)}), f32[2,128,128]{2,1,0:T(8,128)}) %all-reduce.4.cloned.1.call-update) | async-done | bytes 131088 | tf_op jit(solution)/shard_map/psum | solution.py:27
  45.1 1.2 fusion.59
  46.2 1.5 fusion.7
  47.8 0.0 copy-start.3
  47.8 0.8 copy.57
  48.7 2.2 fusion.51
  50.8 0.0 collective-permute-start
  50.9 27.4 %all-reduce.5 = (bf16[256,448]{0,1:T(8,128)(2,1)S(1)}, bf16[256,576]{0,1:T(8,128)(2,1)}) all-reduce(f32[256,448]{0,1:T(8,128)} %fusion.51, f32[256,576]{0,1:T(8,128)} %fusion.62), channel_id=1, replica_groups=mesh['grp'=2,'sv'=4,'tv'=4] {'tv'}, use_global_device_ids=true, to_apply=%region_4.5 | all-reduce | flops 262144 | bytes 1572864 | tf_op jit(solution)/shard_map/psum | solution.py:140
  78.2 0.0 copy-done.3
  78.2 21.2 %all_gather.58 = bf16[256,1792]{0,1:T(8,128)(2,1)S(1)} all-gather(bf16[256,448]{0,1:T(8,128)(2,1)S(1)} %get-tuple-element.498), channel_id=1, replica_groups=mesh['grp'=2,'sv'=4,'tv'=4] {'sv'}, dimensions={1}, use_global_device_ids=true | all-gather | bytes 1146880 | tf_op jit(solution)/shard_map/all_gather | solution.py:144
  99.4 2.1 fusion.61
  101.5 0.4 select_reduce_fusion.1
  101.9 0.3 fusion.55
  102.2 0.2 fusion.22
  102.4 20.1 %all-gather.8 = f32[16,1,256]{2,1,0:T(1,128)S(1)} all-gather(f32[1,1,256]{2,1,0:T(1,128)S(1)} %bitcast.189), channel_id=4, replica_groups=mesh['grp'=2,'sv'=4,'tv'=4] {'sv','tv'}, dimensions={0}, use_global_device_ids=true | all-gather | bytes 17408 | tf_op jit(solution)/shard_map/all_gather | solution.py:11
  122.5 0.0 all-gather.12.cloned.1.call-update
  122.5 17.8 %all-gather = f32[4096,2]{0,1:T(2,128)S(1)} all-gather(f32[256,2]{0,1:T(2,128)S(1)} %get-tuple-element.461), channel_id=2, replica_groups=mesh['grp'=2,'sv'=4,'tv'=4] {'sv','tv'}, dimensions={0}, use_global_device_ids=true | all-gather | bytes 34816 | tf_op jit(solution)/shard_map/all_gather | solution.py:11
  140.4 18.8 %all-gather.1 = f32[4096,2]{0,1:T(2,128)S(1)} all-gather(f32[256,2]{0,1:T(2,128)S(1)} %get-tuple-element.510), channel_id=3, replica_groups=mesh['grp'=2,'sv'=4,'tv'=4] {'sv','tv'}, dimensions={0}, use_global_device_ids=true | all-gather | bytes 34816 | tf_op jit(solution)/shard_map/all_gather | solution.py:11
  159.1 17.6 %all-gather.3 = f32[4096,2]{0,1:T(2,128)S(1)} all-gather(f32[256,2]{0,1:T(2,128)S(1)} %get-tuple-element.460), channel_id=5, replica_groups=mesh['grp'=2,'sv'=4,'tv'=4] {'sv','tv'}, dimensions={0}, use_global_device_ids=true | all-gather | bytes 34816 | tf_op jit(solution)/shard_map/all_gather | solution.py:11
  176.7 0.0 collective-permute-done
  176.7 0.3 collective-permute-start.1
  177.1 1.6 while.42
  178.7 4.5 %collective-permute-done.1 = bf16[256,576]{0,1:T(8,128)(2,1)} collective-permute-done((bf16[256,576]{0,1:T(8,128)(2,1)}, bf16[256,576]{0,1:T(8,128)(2,1)}, u32[]{:S(2)}, u32[]{:S(2)}) %collective-permute-start.1) | collective-permute-done | bytes 294944 | tf_op jit(solution)/shard_map/ppermute | solution.py:131
  183.2 0.0 collective-permute-start.2
  183.2 0.6 fusion.58
  183.8 0.5 slice.101
  184.3 0.6 fusion.57
  184.9 4.6 %collective-permute-done.2 = bf16[256,576]{0,1:T(8,128)(2,1)S(1)} collective-permute-done((bf16[256,576]{0,1:T(8,128)(2,1)}, bf16[256,576]{0,1:T(8,128)(2,1)S(1)}, u32[]{:S(2)}, u32[]{:S(2)}) %collective-permute-start.2) | collective-permute-done | bytes 294944 | tf_op jit(solution)/shard_map/ppermute | solution.py:131
  189.6 1.0 constant_dynamic-update-slice_fusion.6
  190.6 1.0 constant_dynamic-update-slice_fusion.5
  191.5 1.0 constant_dynamic-update-slice_fusion.4
  192.6 1.0 constant_dynamic-update-slice_fusion.2
  193.6 1.0 constant_dynamic-update-slice_fusion.1
  194.5 0.0 copy-done.4
  194.6 1.6 fusion.5
  196.3 2.1 fusion.63
  198.4 0.4 select_reduce_fusion
  198.8 18.7 %all-gather.4 = f32[4096,2]{0,1:T(2,128)S(1)} all-gather(f32[256,2]{0,1:T(2,128)S(1)} %get-tuple-element.459), channel_id=6, replica_groups=mesh['grp'=2,'sv'=4,'tv'=4] {'sv','tv'}, dimensions={0}, use_global_device_ids=true | all-gather | bytes 34816 | tf_op jit(solution)/shard_map/all_gather | solution.py:11
  217.5 0.3 fusion.54
  217.8 0.2 fusion.20
  218.0 17.5 %all-gather.9 = f32[16,1,256]{2,1,0:T(1,128)S(1)} all-gather(f32[1,1,256]{2,1,0:T(1,128)S(1)} %bitcast.190), channel_id=8, replica_groups=mesh['grp'=2,'sv'=4,'tv'=4] {'sv','tv'}, dimensions={0}, use_global_device_ids=true | all-gather | bytes 17408 | tf_op jit(solution)/shard_map/all_gather | solution.py:11
  235.5 18.7 %all-gather.5 = f32[4096,2]{0,1:T(2,128)S(1)} all-gather(f32[256,2]{0,1:T(2,128)S(1)} %get-tuple-element.508), channel_id=7, replica_groups=mesh['grp'=2,'sv'=4,'tv'=4] {'sv','tv'}, dimensions={0}, use_global_device_ids=true | all-gather | bytes 34816 | tf_op jit(solution)/shard_map/all_gather | solution.py:11
  254.3 17.6 %all-gather.7 = f32[4096,2]{0,1:T(2,128)S(1)} all-gather(f32[256,2]{0,1:T(2,128)S(1)} %get-tuple-element.458), channel_id=9, replica_groups=mesh['grp'=2,'sv'=4,'tv'=4] {'sv','tv'}, dimensions={0}, use_global_device_ids=true | all-gather | bytes 34816 | tf_op jit(solution)/shard_map/all_gather | solution.py:11
  271.9 1.5 while.43
  273.5 1.5 subtract_exponential_fusion.2
  275.0 0.0 copy-start.6
  275.0 0.0 copy-start.8
  275.1 1.8 fusion.13
  276.9 0.0 copy-done.8
  276.9 0.6 fusion.39
  (195 shorter events, 2.0 us)
Async XLA Ops:
  7.2 187.4 %copy-start = (bf16[2304,512]{1,0:T(8,128)(2,1)S(1)}, bf16[2304,512]{1,0:T(8,128)(2,1)}, u32[]{:S(2)}) copy-start(bf16[2304,512]{1,0:T(8,128)(2,1)} %param.27) | copy-start | bytes 7077892
  7.2 16.8 %copy-start.12 = (s32[256]{0:T(256)S(1)}, s32[256]{0:T(256)}, u32[]{:S(2)}) copy-start(s32[256]{0:T(256)} %param.21) | copy-start | bytes 3076
  7.2 16.8 %copy-start.13 = (s32[256]{0:T(256)S(1)}, s32[256]{0:T(256)}, u32[]{:S(2)}) copy-start(s32[256]{0:T(256)} %param.20) | copy-start | bytes 3076
  7.2 16.8 %copy-start.14 = (s32[2]{0:T(128)S(1)}, s32[2]{0:T(128)}, u32[]{:S(2)}) copy-start(s32[2]{0:T(128)} %param.22) | copy-start | bytes 28
  7.2 37.9 %all-reduce.4.cloned.1.call-start = ((), (), s32[]{:S(2)}) async-start(), calls=%async_computation | async-start | bytes 262144 | tf_op jit(solution)/shard_map/psum | solution.py:27
  9.1 187.2 %all-gather.12.cloned.1.call-start = ((), (), s32[]{:S(2)}) async-start(), calls=%async_computation.1 | async-start | bytes 1474560 | tf_op jit(solution)/shard_map/all_gather | solution.py:143
  21.5 23.5 %copy-start.16 = (s32[2]{0:T(128)S(1)}, s32[2]{0:T(128)}, u32[]{:S(2)}) copy-start(s32[2]{0:T(128)} %param.23) | copy-start | bytes 28
  21.5 24.7 %copy-start.15 = (bf16[256,576]{0,1:T(8,128)(2,1)S(1)}, bf16[256,576]{0,1:T(8,128)(2,1)}, u32[]{:S(2)}) copy-start(bf16[256,576]{0,1:T(8,128)(2,1)} %param.17) | copy-start | bytes 884740
  24.1 21.0 %copy-start.5 = (s32[256]{0:T(256)}, s32[256]{0:T(256)S(1)}, u32[]{:S(2)}) copy-start(s32[256]{0:T(256)S(1)} %fusion.37) | copy-start | bytes 3076
  47.8 30.4 %copy-start.3 = (bf16[2,72,8,128]{3,2,1,0:T(8,128)(2,1)}, bf16[2,72,8,128]{3,2,1,0:T(8,128)(2,1)S(1)}, u32[]{:S(2)}) copy-start(bf16[2,72,8,128]{3,2,1,0:T(8,128)(2,1)S(1)} %fusion.7) | copy-start | bytes 884740
  50.8 125.9 %collective-permute-start = (bf16[256,576]{0,1:T(8,128)(2,1)}, bf16[256,576]{0,1:T(8,128)(2,1)}, u32[]{:S(2)}, u32[]{:S(2)}) collective-permute-start(bf16[256,576]{0,1:T(8,128)(2,1)} %bitcast.133), channel_id=1, source_target_pairs={{0,1},{1,2},{2,3},{3,0},{4,5},{5,6},{6,7},{7,4},{8,9},{9,10},{10,1... | collective-permute-start | bytes 884744 | tf_op jit(solution)/shard_map/ppermute | solution.py:131
  176.7 6.5 %collective-permute-start.1 = (bf16[256,576]{0,1:T(8,128)(2,1)}, bf16[256,576]{0,1:T(8,128)(2,1)}, u32[]{:S(2)}, u32[]{:S(2)}) collective-permute-start(bf16[256,576]{0,1:T(8,128)(2,1)} %collective-permute-done), channel_id=1, source_target_pairs={{0,1},{1,2},{2,3},{3,0},{4,5},{5,6},{6,7},{7,4},{8,9},{9,10},{10,1... | collective-permute-start | bytes 884744 | tf_op jit(solution)/shard_map/ppermute | solution.py:131
  178.6 15.9 %copy-start.4 = (bf16[2,72,8,128]{3,2,1,0:T(8,128)(2,1)S(1)}, bf16[2,72,8,128]{3,2,1,0:T(8,128)(2,1)}, u32[]{:S(2)}) copy-start(bf16[2,72,8,128]{3,2,1,0:T(8,128)(2,1)} %copy-done.3) | copy-start | bytes 884740
  183.2 6.4 %collective-permute-start.2 = (bf16[256,576]{0,1:T(8,128)(2,1)}, bf16[256,576]{0,1:T(8,128)(2,1)S(1)}, u32[]{:S(2)}, u32[]{:S(2)}) collective-permute-start(bf16[256,576]{0,1:T(8,128)(2,1)} %collective-permute-done.1), channel_id=1, source_target_pairs={{0,1},{1,2},{2,3},{3,0},{4,5},{5,6},{6,7},{7,4},{8,9},{9,10},{10,1... | collective-permute-start | bytes 884744 | tf_op jit(solution)/shard_map/ppermute | solution.py:131
  196.3 2.1 copy-start.1
  198.4 19.6 %copy-start.2 = (f32[256,512]{1,0:T(8,128)}, f32[256,512]{1,0:T(8,128)S(1)}, u32[]{:S(2)}) copy-start(f32[256,512]{1,0:T(8,128)S(1)} %fusion.63) | copy-start | bytes 1572868
  275.0 1.9 copy-start.6
  275.0 1.9 copy-start.7
  275.0 1.8 copy-start.8
  275.0 1.8 copy-start.9
  275.0 1.8 copy-start.10
  275.1 1.8 copy-start.11
Sparse Core Ops, SparseCore 0:
  10.9 34.0 all-reduce.3
  122.7 27.3 all-gather.11
